TPU v7x, 128 devices: a whole 4x4x4 slice. The times are simulated.
128 devices in a mesh: seq: 8 (over z, core), blk: 4 (over y), tp: 4 (over x).
Axes of the slice: x: 4, y: 4, z: 4, core: 2. Of those that a mesh axis runs over, the one named last changes fastest.
Arguments:
- hidden_in: bfloat16 [16384, 1024], P(('seq', 'blk', 'tp')), may hold values from -24 to 24
- ln1_gain: float32 [1024], replicated, may hold values from 0.1 to 1.9
- ln1_bias: float32 [1024], replicated, may hold values from -3 to 3
- qkv_weight: bfloat16 [1024, 3072], replicated, may hold values from -0.1875 to 0.1875
- qv_bias: float32 [2, 1024], replicated, may hold values from -3 to 3
- out_weight: bfloat16 [1024, 1024], replicated, may hold values from -0.75 to 0.75
- out_bias: float32 [1024], replicated, may hold values from -3 to 3
- ln2_gain: float32 [1024], replicated, may hold values from 0.1 to 1.9
- ln2_bias: float32 [1024], replicated, may hold values from -3 to 3
- fc_weight: bfloat16 [1024, 4096], P(None, 'tp'), may hold values from -0.1875 to 0.1875
- fc_bias: float32 [4096], P('tp'), may hold values from -3 to 3
- proj_weight: bfloat16 [4096, 1024], P('tp'), may hold values from -0.09375 to 0.09375
- proj_bias: float32 [1024], replicated, may hold values from -3 to 3
- cotangent: float32 [16384, 1024], P(('seq', 'blk', 'tp')), may hold values from -3 to 3
Outputs:
- block_out: float32 [16384, 1024], P(('seq', 'blk', 'tp'))
- input_grad: float32 [16384, 1024], P(('seq', 'blk', 'tp'))
- ln1_gain_grad: float32 [1024], P(('seq', 'blk'))
- ln1_bias_grad: float32 [1024], P(('seq', 'blk'))
- qkv_weight_grad: float32 [1024, 3072], P(('seq', 'blk'))
- qv_bias_grad: float32 [2, 1024], P(None, ('seq', 'blk'))
- out_weight_grad: float32 [1024, 1024], P(('seq', 'blk'))
- out_bias_grad: float32 [1024], P(('seq', 'blk'))
- ln2_gain_grad: float32 [1024], P(('seq', 'blk'))
- ln2_bias_grad: float32 [1024], P(('seq', 'blk'))
- fc_weight_grad: float32 [1024, 4096], P(None, 'tp')
- fc_bias_grad: float32 [4096], P('tp')
- proj_weight_grad: float32 [4096, 1024], P('tp')
- proj_bias_grad: float32 [1024], P(('seq', 'blk'))
All inputs are finite; a program needn't handle non-finite values.
Results may differ from a plain program's by a relative error of at most 0.025.
Values may be sent and summed in bfloat16 or wider, within the bound.
A program may use at most 128 MiB of HBM per device.

v0:
```python
import math
import jax
import jax.numpy as jnp
from jax import lax
from jax.sharding import PartitionSpec as P

HEADS = 16
HEAD_DIM = 64
epsilon = 1e-05
gelu_coef = math.sqrt(2.0 / math.pi)
masked_score = -1e30


def normalize(matrix, norm_gain, norm_shift):
    row_mean = jnp.mean(matrix, axis=-1, keepdims=True)
    centered = matrix - row_mean
    variance = jnp.mean(centered * centered, axis=-1, keepdims=True)
    inverse = lax.rsqrt(variance + epsilon)
    scaled = centered * inverse
    return (scaled, inverse, scaled * norm_gain + norm_shift)


def norm_back(upstream_grad, scaled, inverse, norm_gain):
    weighted = upstream_grad * norm_gain
    first_mean = jnp.mean(weighted, axis=-1, keepdims=True)
    second_mean = jnp.mean(weighted * scaled, axis=-1, keepdims=True)
    return inverse * (weighted - first_mean - scaled * second_mean)


def gelu_pair(hidden_pre):
    tanh_arg = gelu_coef * (hidden_pre + 0.044715 * hidden_pre * hidden_pre * hidden_pre)
    tanh_value = jnp.tanh(tanh_arg)
    gelu_value = 0.5 * hidden_pre * (1.0 + tanh_value)
    gelu_slope = 0.5 * (1.0 + tanh_value) + 0.5 * hidden_pre * (
        1.0 - tanh_value * tanh_value
    ) * gelu_coef * (1.0 + 3.0 * 0.044715 * hidden_pre * hidden_pre)
    return (gelu_value, gelu_slope)


def per_device(
    hidden_in,
    ln1_gain,
    ln1_bias,
    qkv_weight,
    qv_bias,
    out_weight,
    out_bias,
    ln2_gain,
    ln2_bias,
    fc_weight,
    fc_bias,
    proj_weight,
    proj_bias,
    cotangent,
):
    local_tokens, model_width = hidden_in.shape
    seq_count = lax.axis_size("seq")
    cycle_size = lax.axis_size(("blk", "tp"))
    local_heads = HEADS // seq_count
    head_dim = HEAD_DIM
    query_rows = seq_count * local_tokens
    head_cols = model_width // seq_count
    score_scale = 1.0 / math.sqrt(head_dim)
    hidden_f = hidden_in.astype(jnp.float32)
    scaled_one, inverse_one, normed_one = normalize(hidden_f, ln1_gain, ln1_bias)
    normed_bf = normed_one.astype(jnp.bfloat16)
    weight_three = qkv_weight.reshape(model_width, 3, model_width)
    bias_three = jnp.stack([qv_bias[0], jnp.zeros_like(qv_bias[0]), qv_bias[1]])
    projected = jnp.einsum(
        "td,dcf->ctf", normed_bf, weight_three, preferred_element_type=jnp.float32
    )
    qkv_tokens = (projected + bias_three[:, None, :]).astype(jnp.bfloat16)
    qkv_heads = lax.all_to_all(qkv_tokens, "seq", split_axis=2, concat_axis=1, tiled=True)
    query_heads = qkv_heads[0]
    key_heads = qkv_heads[1]
    value_heads = qkv_heads[2]
    cycle_index = lax.axis_index(("blk", "tp"))
    local_index = jnp.arange(query_rows, dtype=jnp.int32)
    query_place = (
        local_index // local_tokens * cycle_size + cycle_index
    ) * local_tokens + local_index % local_tokens

    def key_positions(first_key, key_count):
        gathered = first_key + jnp.arange(key_count, dtype=jnp.int32)
        within = gathered % query_rows
        return (
            within // local_tokens * cycle_size + gathered // query_rows
        ) * local_tokens + within % local_tokens

    def split_heads(matrix):
        return matrix.reshape(matrix.shape[0], local_heads, head_dim)

    def block_scores(low_row, key_block):
        return (
            jnp.einsum(
                "qhd,khd->hqk",
                split_heads(query_heads[low_row:]),
                split_heads(key_block),
                preferred_element_type=jnp.float32,
            )
            * score_scale
        )

    def visible_of(low_row, key_block, first_key):
        return (
            query_place[low_row:, None] >= key_positions(first_key, key_block.shape[0])[None, :]
        )[None]

    def forward_update(softmax_state, key_block, value_block, first_key, low_row):
        run_max, run_sum, run_acc = softmax_state
        visible = visible_of(low_row, key_block, first_key)
        scores = jnp.where(visible, block_scores(low_row, key_block), masked_score)
        old_max = run_max[:, low_row:]
        new_max = jnp.maximum(old_max, jnp.max(scores, axis=2))
        rescale = jnp.exp(old_max - new_max)
        attn_prob = jnp.where(visible, jnp.exp(scores - new_max[:, :, None]), 0.0)
        new_sum = run_sum[:, low_row:] * rescale + jnp.sum(attn_prob, axis=2)
        weighted_values = jnp.einsum(
            "hqk,khd->qhd",
            attn_prob.astype(jnp.bfloat16),
            split_heads(value_block),
            preferred_element_type=jnp.float32,
        ).reshape(query_rows - low_row, head_cols)
        new_acc = run_acc[low_row:] * jnp.repeat(rescale.T, head_dim, axis=1) + weighted_values
        return (
            run_max.at[:, low_row:].set(new_max),
            run_sum.at[:, low_row:].set(new_sum),
            run_acc.at[low_row:].set(new_acc),
        )

    def by_segments(update, carry_state, key_shard, value_shard, first_key):
        for segment in range(seq_count):
            low_row = segment * local_tokens
            carry_state = update(
                carry_state,
                key_shard[low_row : low_row + local_tokens],
                value_shard[low_row : low_row + local_tokens],
                first_key + low_row,
                low_row,
            )
        return carry_state

    def fold_with(update, carry_state, shard_pair):
        key_piece, value_piece = shard_pair
        piece_rows = key_piece.shape[0]

        def shard_step(shard_number, inner_state):
            offset = shard_number * query_rows
            key_shard = lax.dynamic_slice_in_dim(key_piece, offset, query_rows, 0)
            value_shard = lax.dynamic_slice_in_dim(value_piece, offset, query_rows, 0)
            return by_segments(update, inner_state, key_shard, value_shard, offset)

        return lax.fori_loop(0, piece_rows // query_rows, shard_step, carry_state)

    initial_state = (
        jnp.full((local_heads, query_rows), masked_score, jnp.float32),
        jnp.zeros((local_heads, query_rows), jnp.float32),
        jnp.zeros((query_rows, head_cols), jnp.float32),
    )
    cycle_init = (initial_state,)
    run_max, run_sum, run_acc = fold_with(
        forward_update,
        cycle_init[0],
        (
            lax.all_gather(key_heads, ("blk", "tp"), axis=0, tiled=True),
            lax.all_gather(value_heads, ("blk", "tp"), axis=0, tiled=True),
        ),
    )
    context_heads = (run_acc / jnp.repeat(run_sum.T, head_dim, axis=1)).astype(jnp.bfloat16)
    log_total = run_max + jnp.log(run_sum)
    context_tokens = lax.all_to_all(context_heads, "seq", split_axis=0, concat_axis=1, tiled=True)
    residual = (
        hidden_f
        + jnp.dot(context_tokens, out_weight, preferred_element_type=jnp.float32)
        + out_bias
    )
    scaled_two, inverse_two, normed_two = normalize(residual, ln2_gain, ln2_bias)
    normed_two_bf = normed_two.astype(jnp.bfloat16)
    gathered_norm = lax.all_gather(normed_two_bf, "tp", axis=0, tiled=True)
    hidden_pre = jnp.dot(gathered_norm, fc_weight, preferred_element_type=jnp.float32) + fc_bias
    gelu_value, gelu_slope = gelu_pair(hidden_pre)
    activation = gelu_value.astype(jnp.bfloat16)
    mlp_out = lax.psum_scatter(
        jnp.dot(activation, proj_weight, preferred_element_type=jnp.float32).astype(jnp.bfloat16),
        "tp",
        scatter_dimension=0,
        tiled=True,
    ).astype(jnp.float32)
    block_out = residual + mlp_out + proj_bias
    cot_bf = cotangent.astype(jnp.bfloat16)
    gathered_cot = lax.all_gather(cot_bf, "tp", axis=0, tiled=True)
    hidden_grad = (
        jnp.dot(gathered_cot, proj_weight.T, preferred_element_type=jnp.float32) * gelu_slope
    )
    hidden_grad_bf = hidden_grad.astype(jnp.bfloat16)
    proj_weight_grad = jnp.einsum(
        "tf,td->fd", activation, gathered_cot, preferred_element_type=jnp.float32
    )
    fc_weight_grad = jnp.einsum(
        "td,tf->df", gathered_norm, hidden_grad_bf, preferred_element_type=jnp.float32
    )
    fc_bias_grad = jnp.sum(hidden_grad, axis=0)
    normed_two_grad = lax.psum_scatter(
        jnp.dot(hidden_grad_bf, fc_weight.T, preferred_element_type=jnp.float32).astype(
            jnp.bfloat16
        ),
        "tp",
        scatter_dimension=0,
        tiled=True,
    ).astype(jnp.float32)
    residual_grad = cotangent + norm_back(normed_two_grad, scaled_two, inverse_two, ln2_gain)
    residual_grad_bf = residual_grad.astype(jnp.bfloat16)
    context_grad = jnp.dot(
        residual_grad_bf, out_weight.T, preferred_element_type=jnp.float32
    ).astype(jnp.bfloat16)
    context_grad_heads = lax.all_to_all(
        context_grad, "seq", split_axis=1, concat_axis=0, tiled=True
    )
    delta_rows = jnp.sum(
        split_heads(context_grad_heads).astype(jnp.float32)
        * split_heads(context_heads).astype(jnp.float32),
        axis=2,
    ).T

    def backward_update(grad_state, key_block, value_block, first_key, low_row):
        query_grad, key_grad, value_grad = grad_state
        visible = visible_of(low_row, key_block, first_key)
        attn_prob = jnp.where(
            visible, jnp.exp(block_scores(low_row, key_block) - log_total[:, low_row:, None]), 0.0
        )
        grad_rows = split_heads(context_grad_heads[low_row:])
        prob_grad = jnp.einsum(
            "qhd,khd->hqk", grad_rows, split_heads(value_block), preferred_element_type=jnp.float32
        )
        score_grad = (attn_prob * (prob_grad - delta_rows[:, low_row:, None]) * score_scale).astype(
            jnp.bfloat16
        )
        query_part = jnp.einsum(
            "hqk,khd->qhd", score_grad, split_heads(key_block), preferred_element_type=jnp.float32
        ).reshape(query_rows - low_row, head_cols)
        key_part = jnp.einsum(
            "hqk,qhd->khd",
            score_grad,
            split_heads(query_heads[low_row:]),
            preferred_element_type=jnp.float32,
        ).reshape(key_block.shape[0], head_cols)
        value_part = jnp.einsum(
            "hqk,qhd->khd",
            attn_prob.astype(jnp.bfloat16),
            grad_rows,
            preferred_element_type=jnp.float32,
        ).reshape(key_block.shape[0], head_cols)
        return (
            query_grad.at[low_row:].add(query_part),
            lax.dynamic_update_slice_in_dim(key_grad, key_part, first_key, 0),
            lax.dynamic_update_slice_in_dim(value_grad, value_part, first_key, 0),
        )

    grad_init = (
        jnp.zeros((query_rows, head_cols), jnp.float32),
        jnp.zeros((cycle_size * query_rows, head_cols), jnp.float32),
        jnp.zeros((cycle_size * query_rows, head_cols), jnp.float32),
    )
    query_grad, key_grad, value_grad = fold_with(
        backward_update,
        grad_init,
        (
            lax.all_gather(key_heads, ("blk", "tp"), axis=0, tiled=True),
            lax.all_gather(value_heads, ("blk", "tp"), axis=0, tiled=True),
        ),
    )
    key_own, value_own = (
        lax.psum_scatter(
            key_grad.astype(jnp.bfloat16), ("blk", "tp"), scatter_dimension=0, tiled=True
        ).astype(jnp.float32),
        lax.psum_scatter(
            value_grad.astype(jnp.bfloat16), ("blk", "tp"), scatter_dimension=0, tiled=True
        ).astype(jnp.float32),
    )
    head_grads = jnp.stack([query_grad, key_own, value_own]).astype(jnp.bfloat16)
    token_grads = lax.all_to_all(head_grads, "seq", split_axis=1, concat_axis=2, tiled=True)
    query_bias_grad = jnp.sum(token_grads[0].astype(jnp.float32), axis=0)
    value_bias_grad = jnp.sum(token_grads[2].astype(jnp.float32), axis=0)
    normed_one_grad = jnp.einsum(
        "ctf,dcf->td", token_grads, weight_three, preferred_element_type=jnp.float32
    )
    input_grad = residual_grad + norm_back(normed_one_grad, scaled_one, inverse_one, ln1_gain)
    vectors = jnp.stack(
        [
            jnp.sum(normed_one_grad * scaled_one, axis=0),
            jnp.sum(normed_one_grad, axis=0),
            query_bias_grad,
            value_bias_grad,
            jnp.sum(residual_grad, axis=0),
            jnp.sum(normed_two_grad * scaled_two, axis=0),
            jnp.sum(normed_two_grad, axis=0),
            jnp.sum(cotangent, axis=0),
        ],
        axis=1,
    )
    qkv_weight_grad = jnp.einsum(
        "td,ctf->dcf", normed_bf, token_grads, preferred_element_type=jnp.float32
    ).reshape(model_width, 3 * model_width)
    out_weight_grad = jnp.einsum(
        "tc,td->cd", context_tokens, residual_grad_bf, preferred_element_type=jnp.float32
    )
    qkv_part, out_part, vector_part = (
        lax.psum_scatter(
            qkv_weight_grad.astype(jnp.bfloat16), ("seq", "blk"), scatter_dimension=0, tiled=True
        ).astype(jnp.float32),
        lax.psum_scatter(
            out_weight_grad.astype(jnp.bfloat16), ("seq", "blk"), scatter_dimension=0, tiled=True
        ).astype(jnp.float32),
        lax.psum_scatter(
            vectors.astype(jnp.bfloat16), ("seq", "blk"), scatter_dimension=0, tiled=True
        ).astype(jnp.float32),
    )
    qkv_part, out_part, vector_part = (
        lax.psum(qkv_part.astype(jnp.bfloat16), "tp").astype(jnp.float32),
        lax.psum(out_part.astype(jnp.bfloat16), "tp").astype(jnp.float32),
        lax.psum(vector_part.astype(jnp.bfloat16), "tp").astype(jnp.float32),
    )
    fc_weight_grad, fc_bias_grad, proj_weight_grad = (
        lax.psum(fc_weight_grad.astype(jnp.bfloat16), ("seq", "blk")).astype(jnp.float32),
        lax.psum(fc_bias_grad.astype(jnp.bfloat16), ("seq", "blk")).astype(jnp.float32),
        lax.psum(proj_weight_grad.astype(jnp.bfloat16), ("seq", "blk")).astype(jnp.float32),
    )
    qv_bias_grad = jnp.stack([vector_part[:, 2], vector_part[:, 3]])
    return (
        block_out,
        input_grad,
        vector_part[:, 0],
        vector_part[:, 1],
        qkv_part,
        qv_bias_grad,
        out_part,
        vector_part[:, 4],
        vector_part[:, 5],
        vector_part[:, 6],
        fc_weight_grad,
        fc_bias_grad,
        proj_weight_grad,
        vector_part[:, 7],
    )


def solution(mesh):
    return jax.shard_map(
        per_device,
        mesh=mesh,
        in_specs=(
            P(("seq", "blk", "tp"), None),
            P(),
            P(),
            P(),
            P(),
            P(),
            P(),
            P(),
            P(),
            P(None, "tp"),
            P("tp"),
            P("tp", None),
            P(),
            P(("seq", "blk", "tp"), None),
        ),
        out_specs=(
            P(("seq", "blk", "tp"), None),
            P(("seq", "blk", "tp"), None),
            P(("seq", "blk")),
            P(("seq", "blk")),
            P(("seq", "blk"), None),
            P(None, ("seq", "blk")),
            P(("seq", "blk"), None),
            P(("seq", "blk")),
            P(("seq", "blk")),
            P(("seq", "blk")),
            P(None, "tp"),
            P("tp"),
            P("tp", None),
            P(("seq", "blk")),
        ),
        check_vma=False,
    )
```

profile of v0, /device:TPU:0, one launch (start us, length us, event | category | flops | bytes accessed | tf_op | source)
XLA Modules:
  0.0 1488.0 jit_solution(16899424603222186177)
XLA Ops:
  7.2 1.2 convert_reduce_fusion
  8.5 1.2 fusion.217
  10.5 8.7 copy.287
  19.4 5.9 fusion.199
  25.3 2.3 copy.289
  27.6 21.5 %all_to_all.71 = bf16[3,128,1024]{1,0,2:T(4,128)(2,1)S(1)} all-to-all(bf16[3,128,1024]{1,0,2:T(4,128)(2,1)} %copy.289), channel_id=1, replica_groups=mesh['seq'=8,'blk'=4,'tp'=4] {'seq'}, dimensions={2} | all-to-all | bytes 1572864 | tf_op jit(solution)/shard_map/all_to_all | solution.py:73
  49.1 1.1 fusion.253
  57.5 45.0 %all-gather.7.cloned.1.call-done = bf16[16384,128]{0,1:T(8,128)(2,1)} async-done(((bf16[1024,128]{0,1:T(8,128)(2,1)}), bf16[16384,128]{0,1:T(8,128)(2,1)}) %all-gather.7.cloned.1.call-update) | async-done | bytes 4194320 | tf_op jit(solution)/shard_map/all_gather | solution.py:166
  102.5 53.9 %all-gather.5.cloned.1.call-done = bf16[16384,128]{0,1:T(8,128)(2,1)} async-done(((bf16[1024,128]{0,1:T(8,128)(2,1)}), bf16[16384,128]{0,1:T(8,128)(2,1)}) %all-gather.5.cloned.1.call-update) | async-done | bytes 4194320 | tf_op jit(solution)/shard_map/all_gather | solution.py:165
  156.5 220.2 %while.112 = (s32[]{:T(128)}, f32[2,1024]{1,0:T(2,128)S(1)}, f32[2,1024]{1,0:T(2,128)S(1)}, f32[1024,128]{0,1:T(8,128)S(1)}, s32[1024]{0:T(1024)S(1)}, /*index=5...) while((s32[]{:T(128)}, f32[2,1024]{1,0:T(2,128)S(1)}, ...), condition=%wide.region_26.27_spmd, body=%wide.region_9.26_spmd.sunk | while | flops 314464256 | bytes 33136192 | solution.py:153
  171.6 1.1 constant_dynamic-slice_fusion.35
  185.3 1.1 constant_dynamic-slice_fusion.35
  199.1 1.1 constant_dynamic-slice_fusion.35
  212.9 1.1 constant_dynamic-slice_fusion.35
  226.6 1.1 constant_dynamic-slice_fusion.35
  240.4 1.1 constant_dynamic-slice_fusion.35
  254.1 1.1 constant_dynamic-slice_fusion.35
  267.9 1.1 constant_dynamic-slice_fusion.35
  281.7 1.1 constant_dynamic-slice_fusion.35
  295.4 1.1 constant_dynamic-slice_fusion.35
  377.4 1.1 copy.294
  378.6 11.8 all_to_all.72
  391.2 2.2 fusion.256
  394.6 2.0 fusion.254
  396.8 19.6 %all-gather.9.cloned.1.call-done = bf16[512,1024]{1,0:T(8,128)(2,1)} async-done(((bf16[128,1024]{1,0:T(8,128)(2,1)}), bf16[512,1024]{1,0:T(8,128)(2,1)}) %all-gather.9.cloned.1.call-update) | async-done | bytes 1048592 | tf_op jit(solution)/shard_map/all_gather | solution.py:179
  416.4 4.6 fusion.274
  420.9 21.8 %all-gather.11.cloned.1.call-done = bf16[512,1024]{1,0:T(8,128)(2,1)} async-done(((bf16[128,1024]{1,0:T(8,128)(2,1)}), bf16[512,1024]{1,0:T(8,128)(2,1)}) %all-gather.11.cloned.1.call-update) | async-done | bytes 1048592 | tf_op jit(solution)/shard_map/all_gather | solution.py:191
  442.8 4.4 fusion.257
  448.2 2.3 convolution_convert_fusion.4
  450.6 4.1 convolution_convert_fusion.5
  454.7 19.8 %reduce-scatter.12.cloned.1.call-done = bf16[128,1024]{1,0:T(8,128)(2,1)} async-done(((bf16[512,1024]{1,0:T(8,128)(2,1)}), bf16[128,1024]{1,0:T(8,128)(2,1)}) %reduce-scatter.12.cloned.1.call-update) | async-done | bytes 262160 | tf_op jit(solution)/shard_map/reduce_scatter | solution.py:203
  474.5 1.2 fusion.222
  475.8 25.0 %reduce-scatter.10.cloned.1.call-done = bf16[128,1024]{1,0:T(8,128)(2,1)} async-done(((bf16[512,1024]{1,0:T(8,128)(2,1)}), bf16[128,1024]{1,0:T(8,128)(2,1)}) %reduce-scatter.10.cloned.1.call-update) | async-done | bytes 262160 | tf_op jit(solution)/shard_map/reduce_scatter | solution.py:183
  500.7 2.2 fusion.243
  505.5 4.4 all-to-all-start.2
  510.1 7.3 all-to-all-done.2
  518.3 2.4 broadcast.5700.clone
  520.7 2.4 broadcast.5700
  523.1 378.5 %while.113 = (s32[]{:T(128)}, f32[1024,128]{0,1:T(8,128)S(1)}, bf16[16384,128]{0,1:T(8,128)(2,1)}, bf16[16384,128]{0,1:T(8,128)(2,1)}, bf16[16384,128]{0,1:T(8,1...) while((s32[]{:T(128)}, f32[1024,128]{0,1:T(8,128)S(1)}, ...), condition=%wide.region_35.36_spmd, body=%wide.region_34.35_spmd.sunk | while | flops 765635584 | bytes 45661068 | solution.py:153
  901.6 6.4 copy.302
  908.1 6.4 copy.301
  915.8 4.0 convolution_convert_fusion.2
  919.8 3.0 convolution_convert_fusion.1
  923.0 60.5 %reduce-scatter.16.cloned.1.call-done = bf16[1024,128]{1,0:T(8,128)(2,1)} async-done(((bf16[16384,128]{1,0:T(8,128)(2,1)}), bf16[1024,128]{1,0:T(8,128)(2,1)}) %reduce-scatter.16.cloned.1.call-update) | async-done | bytes 262160 | tf_op jit(solution)/shard_map/reduce_scatter | solution.py:276
  983.5 81.2 %reduce-scatter.14.cloned.1.call-done = bf16[1024,128]{1,0:T(8,128)(2,1)} async-done(((bf16[16384,128]{1,0:T(8,128)(2,1)}), bf16[1024,128]{1,0:T(8,128)(2,1)}) %reduce-scatter.14.cloned.1.call-update) | async-done | bytes 262160 | tf_op jit(solution)/shard_map/reduce_scatter | solution.py:273
  1064.7 1.1 pad_maximum_fusion
  1065.8 1.6 copy.303
  1067.5 4.4 all-to-all-start.3
  1072.1 19.8 %all-to-all-done.3 = bf16[3,1024,128]{2,0,1:T(4,128)(2,1)S(1)} async-done(((bf16[3,1024,128]{2,0,1:T(4,128)(2,1)}), bf16[3,1024,128]{2,0,1:T(4,128)(2,1)S(1)}, u32[]{:S(2)}, u32[]{:S(2)}) %all-to-all-start.3) | async-done | bytes 786464 | tf_op jit(solution)/shard_map/all_to_all | solution.py:281
  1092.9 1.9 copy.355
  1095.3 4.2 fusion.216
  1100.6 2.0 convolution_convert_fusion.3
  1103.3 4.6 convolution_convert_fusion
  1108.0 64.7 %psum.46 = bf16[1024]{0:T(1024)(128)(2,1)S(1)} all-reduce(bf16[1024]{0:T(1024)(128)(2,1)S(1)} %get-tuple-element.1920), channel_id=1, replica_groups=mesh['seq'=8,'blk'=4,'tp'=4] {'seq','blk'}, use_global_device_ids=true, to_apply=%region_56.57 | all-reduce | flops 1024 | bytes 4096 | tf_op jit(solution)/shard_map/psum | solution.py:325
  1173.2 10.0 all-reduce.5.cloned.1.call-done
  1183.2 4.2 convert_element_type.415
  1187.4 2.5 convert_element_type.419
  1190.9 72.7 %reduce-scatter.22.cloned.1.call-done = bf16[32,8]{1,0:T(8,128)(2,1)} async-done(((bf16[1024,8]{1,0:T(8,128)(2,1)}), bf16[32,8]{1,0:T(8,128)(2,1)}) %reduce-scatter.22.cloned.1.call-update) | async-done | bytes 528
  1264.4 10.4 psum.42
  1274.8 70.6 %reduce-scatter.20.cloned.1.call-done = bf16[32,1024]{1,0:T(8,128)(2,1)} async-done(((bf16[1024,1024]{1,0:T(8,128)(2,1)}), bf16[32,1024]{1,0:T(8,128)(2,1)}) %reduce-scatter.20.cloned.1.call-update) | async-done | bytes 65552 | tf_op jit(solution)/shard_map/reduce_scatter | solution.py:311
  1345.4 89.2 %reduce-scatter.18.cloned.1.call-done = bf16[32,3072]{1,0:T(8,128)(2,1)} async-done(((bf16[1024,3072]{1,0:T(8,128)(2,1)}), bf16[32,3072]{1,0:T(8,128)(2,1)}) %reduce-scatter.18.cloned.1.call-update) | async-done | bytes 196624 | tf_op jit(solution)/shard_map/reduce_scatter | solution.py:308
  1435.7 42.4 %all-reduce.7.cloned.1.call-done = (bf16[32,3072]{1,0:T(8,128)(2,1)}, bf16[32,1024]{1,0:T(8,128)(2,1)}) async-done(((bf16[32,3072]{1,0:T(8,128)(2,1)}, bf16[32,1024]{1,0:T(8,128)(2,1)}), (bf16[32,3072]{1,0:T(8,128)(2,1)}, bf16[32,1024]{1,0:T(8,128)(2,1)})) %all-reduce.7.cloned.1.call-update) | async-done | bytes 262160 | tf_op jit(solution)/shard_map/psum | solution.py:319
  1478.1 1.5 convert_element_type.413
  1479.6 1.7 convert_element_type.411
  (3209 shorter events, 594.2 us)
Async XLA Ops:
  7.2 435.6 %copy-start = (bf16[1024,1024]{1,0:T(8,128)(2,1)S(1)}, bf16[1024,1024]{1,0:T(8,128)(2,1)}, u32[]{:S(2)}) copy-start(bf16[1024,1024]{1,0:T(8,128)(2,1)} %param.101) | copy-start | bytes 6291460
  7.2 95.3 %all-gather.7.cloned.1.call-start = ((), (), s32[]{:S(2)}) async-start(), calls=%async_computation.12 | async-start | bytes 4456448 | tf_op jit(solution)/shard_map/all_gather | solution.py:166
  8.5 10.9 copy-start.16
  9.6 9.7 copy-start.18
  10.4 8.9 copy-start.2
  10.4 8.9 copy-start.11
  10.5 8.9 copy-start.13
  51.4 105.1 %all-gather.5.cloned.1.call-start = ((), (), s32[]{:S(2)}) async-start(), calls=%async_computation.11 | async-start | bytes 4456448 | tf_op jit(solution)/shard_map/all_gather | solution.py:165
  52.5 363.9 %all-gather.9.cloned.1.call-start = ((), (), s32[]{:S(2)}) async-start(), calls=%async_computation.13 | async-start | bytes 1310720 | tf_op jit(solution)/shard_map/all_gather | solution.py:179
  376.7 14.5 copy-start.20
  390.3 3.3 copy-start.15
  390.3 3.4 copy-start.21
  394.6 48.2 %all-gather.11.cloned.1.call-start = ((), (), s32[]{:S(2)}) async-start(), calls=%async_computation.15 | async-start | bytes 1310720 | tf_op jit(solution)/shard_map/all_gather | solution.py:191
  396.7 46.1 %copy-start.26 = (f32[1024]{0:T(1024)S(1)}, f32[1024]{0:T(1024)}, u32[]{:S(2)}) copy-start(f32[1024]{0:T(1024)} %param.100) | copy-start | bytes 12292
  396.7 77.8 %reduce-scatter.12.cloned.1.call-start = ((), (), s32[]{:S(2)}) async-start(), calls=%async_computation.16 | async-start | bytes 1310720 | tf_op jit(solution)/shard_map/reduce_scatter | solution.py:203
  442.8 5.4 copy-start.23
  447.2 1.0 copy-start.28
  450.5 50.2 %copy-start.22 = (f32[1024]{0:T(1024)S(1)}, f32[1024]{0:T(1024)}, u32[]{:S(2)}) copy-start(f32[1024]{0:T(1024)} %param.102) | copy-start | bytes 12292
  450.5 50.2 %reduce-scatter.10.cloned.1.call-start = ((), (), s32[]{:S(2)}) async-start(), calls=%async_computation.14 | async-start | bytes 1310720 | tf_op jit(solution)/shard_map/reduce_scatter | solution.py:183
  454.7 49.1 %copy-start.3 = (bf16[1024,1024]{1,0:T(8,128)(2,1)S(1)}, bf16[1024,1024]{1,0:T(8,128)(2,1)}, u32[]{:S(2)}) copy-start(bf16[1024,1024]{1,0:T(8,128)(2,1)} %param.95) | copy-start | bytes 6291460
  503.0 0.8 copy-start.4
  505.5 12.0 all-to-all-start.2
  509.9 8.3 copy-start.8
  509.9 473.6 %reduce-scatter.16.cloned.1.call-start = ((), (), s32[]{:S(2)}) async-start(), calls=%async_computation.18 | async-start | bytes 4456448 | tf_op jit(solution)/shard_map/reduce_scatter | solution.py:276
  908.0 156.7 %reduce-scatter.14.cloned.1.call-start = ((), (), s32[]{:S(2)}) async-start(), calls=%async_computation.17 | async-start | bytes 4456448 | tf_op jit(solution)/shard_map/reduce_scatter | solution.py:273
  914.4 1.4 copy-start.24
  914.5 268.7 %all-reduce.5.cloned.1.call-start = ((), (), s32[]{:S(2)}) async-start(), calls=%async_computation.22 | async-start | bytes 8388608 | tf_op jit(solution)/shard_map/psum | solution.py:324
  915.8 4.0 copy-start.25
  915.8 4.0 copy-start.27
  1065.8 6.1 copy-start.7
  1067.5 24.5 %all-to-all-start.3 = ((bf16[3,1024,128]{2,0,1:T(4,128)(2,1)}), bf16[3,1024,128]{2,0,1:T(4,128)(2,1)S(1)}, u32[]{:S(2)}, u32[]{:S(2)}) async-start(bf16[3,1024,128]{2,0,1:T(4,128)(2,1)} %copy.303), calls=%async_computation.7 | async-start | bytes 2097152 | tf_op jit(solution)/shard_map/all_to_all | solution.py:281
  1071.9 191.8 %reduce-scatter.22.cloned.1.call-start = ((), (), s32[]{:S(2)}) async-start(), calls=%async_computation.21 | async-start | bytes 270336
  1072.0 23.3 %copy-start.12 = (f32[1024]{0:T(1024)S(1)}, f32[1024]{0:T(1024)}, u32[]{:S(2)}) copy-start(f32[1024]{0:T(1024)} %param.91) | copy-start | bytes 12292
  1072.0 23.3 %copy-start.17 = (f32[128]{0:T(128)S(1)}, f32[128]{0:T(128)}, u32[]{:S(2)}) copy-start(f32[128]{0:T(128)} %copy-done.16) | copy-start | bytes 1540
  1072.0 23.3 %copy-start.19 = (f32[128]{0:T(128)S(1)}, f32[128]{0:T(128)}, u32[]{:S(2)}) copy-start(f32[128]{0:T(128)} %copy-done.18) | copy-start | bytes 1540
  1091.9 1.0 copy-start.6
  1095.3 5.2 copy-start.5
  1095.3 5.2 copy-start.9
  1100.5 244.9 %reduce-scatter.20.cloned.1.call-start = ((), (), s32[]{:S(2)}) async-start(), calls=%async_computation.20 | async-start | bytes 2162688 | tf_op jit(solution)/shard_map/reduce_scatter | solution.py:311
  1102.6 0.7 copy-start.14
  1102.6 331.9 %reduce-scatter.18.cloned.1.call-start = ((), (), s32[]{:S(2)}) async-start(), calls=%async_computation.19 | async-start | bytes 6488064 | tf_op jit(solution)/shard_map/reduce_scatter | solution.py:308
  1107.9 370.2 %all-reduce.7.cloned.1.call-start = ((), (), s32[]{:S(2)}) async-start(), calls=%async_computation.23 | async-start | bytes 524288 | tf_op jit(solution)/shard_map/psum | solution.py:319
  1183.2 4.2 copy-start.10
  1187.4 293.9 %copy-start.1 = (bf16[1024,1024]{1,0:T(8,128)(2,1)S(1)}, bf16[1024,1024]{1,0:T(8,128)(2,1)}, u32[]{:S(2)}) copy-start(bf16[1024,1024]{1,0:T(8,128)(2,1)} %param.101) | copy-start | bytes 6291460
Sparse Core Ops, SparseCore 0:
  51.5 50.9 all-gather.6
  105.2 51.1 all-gather.4
  394.7 21.6 all-gather.8
  418.5 24.2 all-gather.10
  450.7 23.8 reduce-scatter.11
  477.5 23.2 reduce-scatter.9
  908.1 75.2 reduce-scatter.15
  987.8 76.8 reduce-scatter.13
  1068.7 114.4 all-reduce.4
  1187.0 76.5 reduce-scatter.21
  1267.2 78.1 reduce-scatter.19
  1349.0 85.5 reduce-scatter.17
  1437.2 40.8 all-reduce.6
where the time goes:
time: 1500 us; the launch traced here: 1490 us
  waiting for transfers between devices  639 us (43%)
  matrix products  276 us (18%)
  local copies, waits for them, and re-layouts  249 us (17%)
  other arithmetic  174 us (12%)
  blocking collectives  108 us (7%)
  loops' own time  17.9 us (1%)
    reduce_scatter x1, waiting for transfers between devices, per_device(): lax.psum_scatter(qkv_weight_grad.astype(jnp.bfloat16), ('seq', 'blk'), sc...  89.2 us
    dot_general x256, matrix products, block_scores(): jnp.einsum('qhd,khd->hqk', split_heads(query_heads[low_row:]), split_head...  82.9 us
    reduce_scatter x1, waiting for transfers between devices, per_device(): lax.psum_scatter(key_grad.astype(jnp.bfloat16), ('blk', 'tp'), scatter_di...  81.2 us
    dynamic_update_slice x128, local copies, waits for them, and re-layouts, backward_update(): lax.dynamic_update_slice_in_dim(value_grad, value_part, first_key, 0)  79.2 us
    scatter x112, other arithmetic, forward_update(): run_sum.at[:, low_row:].set(new_sum)  75 us
    unnamed x14, waiting for transfers between devices  72.9 us
    reduce_scatter x1, waiting for transfers between devices, per_device(): lax.psum_scatter(out_weight_grad.astype(jnp.bfloat16), ('seq', 'blk'), sc...  70.6 us
    dynamic_update_slice x112, local copies, waits for them, and re-layouts, backward_update(): lax.dynamic_update_slice_in_dim(key_grad, key_part, first_key, 0)  69 us
  transfers between devices with their start and end apart: 15, of which 15 were waited for; matrix products, arithmetic and copies ran while one was open for 4% of the time, Pallas kernels for 0%

commit v1 on v0

--- a/solution.py
+++ b/solution.py
@@ -162,7 +162,12 @@
         forward_update,
         cycle_init[0],
         (
-            lax.all_gather(key_heads, ("blk", "tp"), axis=0, tiled=True),
+            jnp.concatenate(
+                lax.all_to_all(
+                    jnp.stack([key_heads] * lax.axis_size(("blk", "tp"))), ("blk", "tp"), 0, 0
+                ),
+                axis=0,
+            ),
             lax.all_gather(value_heads, ("blk", "tp"), axis=0, tiled=True),
         ),
     )

time: 1500 us -> 1940 us (1.29)
  local copies, waits for them, and re-layouts: 249 us -> 565 us
  matrix products: 276 us -> 360 us
    while x16 -> x784, local copies, waits for them, and re-layouts: 0.03 us -> 203 us
    dot_general x256, matrix products: 82.9 us -> 167 us  [block_scores(): jnp.einsum('qhd,khd->hqk', split_heads(query_heads[low_row:]), split_head...]
    slice x224, local copies, waits for them, and re-layouts: 3.17 us -> 76.2 us  [block_scores(): query_heads[low_row:]]
    all_to_all x0 -> x1, waiting for transfers between devices: none -> 66.5 us  [per_device(): lax.all_to_all(jnp.stack([key_heads] * lax.axis_size(('blk', 'tp'))), ('b...]
    all_gather x1, waiting for transfers between devices: 45 us -> 5.51 us  [per_device(): lax.all_gather(value_heads, ('blk', 'tp'), axis=0, tiled=True)]
    slice x16 -> x32, local copies, waits for them, and re-layouts: 14.8 us -> 40.2 us  [by_segments(): key_shard[low_row:low_row + local_tokens]]
where the time goes in v1:
time: 1940 us; the launch traced here: 1920 us
  waiting for transfers between devices  648 us (33%)
  local copies, waits for them, and re-layouts  565 us (29%)
  matrix products  360 us (19%)
  other arithmetic  185 us (10%)
  blocking collectives  106 us (5%)
  loops' own time  20.4 us (1%)
    while x784, local copies, waits for them, and re-layouts  203 us
    dot_general x256, matrix products, block_scores(): jnp.einsum('qhd,khd->hqk', split_heads(query_heads[low_row:]), split_head...  167 us
    reduce_scatter x1, waiting for transfers between devices, per_device(): lax.psum_scatter(qkv_weight_grad.astype(jnp.bfloat16), ('seq', 'blk'), sc...  89.2 us
    reduce_scatter x1, waiting for transfers between devices, per_device(): lax.psum_scatter(key_grad.astype(jnp.bfloat16), ('blk', 'tp'), scatter_di...  81.2 us
    dynamic_update_slice x128, local copies, waits for them, and re-layouts, backward_update(): lax.dynamic_update_slice_in_dim(value_grad, value_part, first_key, 0)  79.2 us
    slice x224, local copies, waits for them, and re-layouts, block_scores(): query_heads[low_row:]  76.2 us
    scatter x112, other arithmetic, forward_update(): run_sum.at[:, low_row:].set(new_sum)  75.7 us
    unnamed x14, waiting for transfers between devices  73.4 us

profile of v1, /device:TPU:0, one launch (start us, length us, event | category | flops | bytes accessed | tf_op | source)
XLA Modules:
  0.0 1917.8 jit_solution(1806991275964906481)
XLA Ops:
  10.5 8.7 copy.287
  19.3 5.0 fusion.199
  25.8 21.5 %all_to_all.76 = bf16[3,128,1024]{1,0,2:T(4,128)(2,1)S(1)} all-to-all(bf16[3,128,1024]{1,0,2:T(4,128)(2,1)} %copy.289), channel_id=1, replica_groups=mesh['seq'=8,'blk'=4,'tp'=4] {'seq'}, dimensions={2} | all-to-all | bytes 1572864 | tf_op jit(solution)/shard_map/all_to_all | solution.py:73
  49.9 2.5 stack.62
  52.5 7.1 all-to-all-start.1
  64.9 66.5 %all-to-all-done.1 = bf16[16,1024,128]{1,2,0:T(8,128)(2,1)} async-done(((bf16[16,1024,128]{1,2,0:T(8,128)(2,1)}), bf16[16,1024,128]{1,2,0:T(8,128)(2,1)}, u32[]{:S(2)}, u32[]{:S(2)}) %all-to-all-start.1) | async-done | bytes 4194336 | tf_op jit(solution)/shard_map/all_to_all | solution.py:166
  131.4 6.4 copy.291
  137.8 5.5 all-gather.5.cloned.1.call-done
  144.0 626.6 %while.112 = (s32[]{:T(128)}, f32[2,1024]{1,0:T(2,128)S(1)}, f32[2,1024]{1,0:T(2,128)}, f32[1024,128]{0,1:T(8,128)S(1)}, s32[1024]{0:T(1024)S(1)}, /*index=5*/bf...) while((s32[]{:T(128)}, f32[2,1024]{1,0:T(2,128)S(1)}, ...), condition=%wide.region_26.27_spmd, body=%wide.region_9.26_spmd.sunk | while | flops 314464256 | bytes 39362704 | solution.py:153
  150.4 1.6 constant_dynamic-slice_fusion.37
  189.6 1.6 constant_dynamic-slice_fusion.37
  228.8 1.6 constant_dynamic-slice_fusion.37
  267.9 1.6 constant_dynamic-slice_fusion.37
  307.1 1.6 constant_dynamic-slice_fusion.37
  346.2 1.6 constant_dynamic-slice_fusion.37
  385.4 1.6 constant_dynamic-slice_fusion.37
  424.5 1.6 constant_dynamic-slice_fusion.37
  463.7 1.6 constant_dynamic-slice_fusion.37
  502.9 1.6 constant_dynamic-slice_fusion.37
  542.0 1.6 constant_dynamic-slice_fusion.37
  581.2 1.6 constant_dynamic-slice_fusion.37
  620.3 1.6 constant_dynamic-slice_fusion.37
  659.5 1.6 constant_dynamic-slice_fusion.37
  773.2 9.9 all_to_all.77
  784.0 2.2 fusion.256
  787.4 2.0 fusion.254
  790.1 18.1 all-gather.7.cloned.1.call-done
  808.2 4.5 fusion.274
  812.7 22.1 %all-gather.9.cloned.1.call-done = bf16[512,1024]{1,0:T(8,128)(2,1)} async-done(((bf16[128,1024]{1,0:T(8,128)(2,1)}), bf16[512,1024]{1,0:T(8,128)(2,1)}) %all-gather.9.cloned.1.call-update) | async-done | bytes 1048592 | tf_op jit(solution)/shard_map/all_gather | solution.py:196
  834.8 5.0 fusion.257
  840.8 2.3 convolution_convert_fusion.4
  843.1 4.1 convolution_convert_fusion.5
  847.8 19.3 %reduce-scatter.12.cloned.1.call-done = bf16[128,1024]{1,0:T(8,128)(2,1)} async-done(((bf16[512,1024]{1,0:T(8,128)(2,1)}), bf16[128,1024]{1,0:T(8,128)(2,1)}) %reduce-scatter.12.cloned.1.call-update) | async-done | bytes 262160 | tf_op jit(solution)/shard_map/reduce_scatter | solution.py:208
  867.1 1.8 fusion.222
  868.9 24.4 %reduce-scatter.10.cloned.1.call-done = bf16[128,1024]{1,0:T(8,128)(2,1)} async-done(((bf16[512,1024]{1,0:T(8,128)(2,1)}), bf16[128,1024]{1,0:T(8,128)(2,1)}) %reduce-scatter.10.cloned.1.call-update) | async-done | bytes 262160 | tf_op jit(solution)/shard_map/reduce_scatter | solution.py:188
  893.2 2.8 fusion.243
  898.5 4.4 all-to-all-start.3
  903.2 7.3 all-to-all-done.3
  911.3 35.2 %all-gather.11.cloned.1.call-done = bf16[16384,128]{0,1:T(8,128)(2,1)} async-done(((bf16[1024,128]{0,1:T(8,128)(2,1)}), bf16[16384,128]{0,1:T(8,128)(2,1)}) %all-gather.11.cloned.1.call-update) | async-done | bytes 4194320 | tf_op jit(solution)/shard_map/all_gather | solution.py:273
  946.6 2.4 broadcast.5701.clone
  949.0 2.4 broadcast.5701
  951.4 378.1 %while.113 = (s32[]{:T(128)}, f32[1024,128]{0,1:T(8,128)S(1)}, bf16[16384,128]{0,1:T(8,128)(2,1)}, bf16[16384,128]{0,1:T(8,128)(2,1)}, bf16[16384,128]{0,1:T(8,1...) while((s32[]{:T(128)}, f32[1024,128]{0,1:T(8,128)S(1)}, ...), condition=%wide.region_35.36_spmd, body=%wide.region_34.35_spmd.sunk | while | flops 765635584 | bytes 45661068 | solution.py:153
  1329.5 6.4 copy.304
  1336.0 6.4 copy.303
  1343.5 4.0 convolution_convert_fusion.2
  1347.5 3.0 convolution_convert_fusion.1
  1350.7 62.5 %reduce-scatter.16.cloned.1.call-done = bf16[1024,128]{1,0:T(8,128)(2,1)} async-done(((bf16[16384,128]{1,0:T(8,128)(2,1)}), bf16[1024,128]{1,0:T(8,128)(2,1)}) %reduce-scatter.16.cloned.1.call-update) | async-done | bytes 262160 | tf_op jit(solution)/shard_map/reduce_scatter | solution.py:281
  1413.2 81.2 %reduce-scatter.14.cloned.1.call-done = bf16[1024,128]{1,0:T(8,128)(2,1)} async-done(((bf16[16384,128]{1,0:T(8,128)(2,1)}), bf16[1024,128]{1,0:T(8,128)(2,1)}) %reduce-scatter.14.cloned.1.call-update) | async-done | bytes 262160 | tf_op jit(solution)/shard_map/reduce_scatter | solution.py:278
  1495.6 1.6 copy.305
  1497.2 4.4 all-to-all-start.4
  1501.9 19.8 %all-to-all-done.4 = bf16[3,1024,128]{2,0,1:T(4,128)(2,1)S(1)} async-done(((bf16[3,1024,128]{2,0,1:T(4,128)(2,1)}), bf16[3,1024,128]{2,0,1:T(4,128)(2,1)S(1)}, u32[]{:S(2)}, u32[]{:S(2)}) %all-to-all-start.4) | async-done | bytes 786464 | tf_op jit(solution)/shard_map/all_to_all | solution.py:286
  1522.9 4.9 fusion.216
  1528.9 2.0 convolution_convert_fusion.3
  1531.6 4.6 convolution_convert_fusion
  1536.9 64.4 %psum.46 = bf16[1024]{0:T(1024)(128)(2,1)S(1)} all-reduce(bf16[1024]{0:T(1024)(128)(2,1)S(1)} %copy-done.48), channel_id=1, replica_groups=mesh['seq'=8,'blk'=4,'tp'=4] {'seq','blk'}, use_global_device_ids=true, to_apply=%region_56.57 | all-reduce | flops 1024 | bytes 4096 | tf_op jit(solution)/shard_map/psum | solution.py:330
  1601.9 11.0 all-reduce.5.cloned.1.call-done
  1612.9 4.2 convert_element_type.415
  1617.2 2.5 convert_element_type.419
  1620.7 72.6 %reduce-scatter.22.cloned.1.call-done = bf16[32,8]{1,0:T(8,128)(2,1)} async-done(((bf16[1024,8]{1,0:T(8,128)(2,1)}), bf16[32,8]{1,0:T(8,128)(2,1)}) %reduce-scatter.22.cloned.1.call-update) | async-done | bytes 528
  1694.1 10.4 psum.42
  1704.6 70.6 %reduce-scatter.20.cloned.1.call-done = bf16[32,1024]{1,0:T(8,128)(2,1)} async-done(((bf16[1024,1024]{1,0:T(8,128)(2,1)}), bf16[32,1024]{1,0:T(8,128)(2,1)}) %reduce-scatter.20.cloned.1.call-update) | async-done | bytes 65552 | tf_op jit(solution)/shard_map/reduce_scatter | solution.py:316
  1775.1 89.2 %reduce-scatter.18.cloned.1.call-done = bf16[32,3072]{1,0:T(8,128)(2,1)} async-done(((bf16[1024,3072]{1,0:T(8,128)(2,1)}), bf16[32,3072]{1,0:T(8,128)(2,1)}) %reduce-scatter.18.cloned.1.call-update) | async-done | bytes 196624 | tf_op jit(solution)/shard_map/reduce_scatter | solution.py:313
  1865.4 42.4 %all-reduce.7.cloned.1.call-done = (bf16[32,3072]{1,0:T(8,128)(2,1)}, bf16[32,1024]{1,0:T(8,128)(2,1)}) async-done(((bf16[32,3072]{1,0:T(8,128)(2,1)}, bf16[32,1024]{1,0:T(8,128)(2,1)}), (bf16[32,3072]{1,0:T(8,128)(2,1)}, bf16[32,1024]{1,0:T(8,128)(2,1)})) %all-reduce.7.cloned.1.call-update) | async-done | bytes 262160 | tf_op jit(solution)/shard_map/psum | solution.py:324
  1909.3 1.7 convert_element_type.411
  (4011 shorter events, 996.8 us)
Async XLA Ops:
  7.2 827.6 %copy-start = (bf16[1024,1024]{1,0:T(8,128)(2,1)S(1)}, bf16[1024,1024]{1,0:T(8,128)(2,1)}, u32[]{:S(2)}) copy-start(bf16[1024,1024]{1,0:T(8,128)(2,1)} %param.101) | copy-start | bytes 6291460
  7.2 136.1 %all-gather.5.cloned.1.call-start = ((), (), s32[]{:S(2)}) async-start(), calls=%async_computation.12 | async-start | bytes 4456448 | tf_op jit(solution)/shard_map/all_gather | solution.py:171
  8.5 10.8 copy-start.39
  9.6 9.7 copy-start.41
  10.4 8.9 copy-start.6
  10.4 8.9 copy-start.34
  10.5 8.9 copy-start.36
  52.5 79.0 %all-to-all-start.1 = ((bf16[16,1024,128]{1,2,0:T(8,128)(2,1)}), bf16[16,1024,128]{1,2,0:T(8,128)(2,1)}, u32[]{:S(2)}, u32[]{:S(2)}) async-start(bf16[16,1024,128]{1,2,0:T(8,128)(2,1)} %stack.62), calls=%async_computation.1 | async-start | bytes 8388608 | tf_op jit(solution)/shard_map/all_to_all | solution.py:166
  59.6 748.6 %all-gather.7.cloned.1.call-start = ((), (), s32[]{:S(2)}) async-start(), calls=%async_computation.13 | async-start | bytes 1310720 | tf_op jit(solution)/shard_map/all_gather | solution.py:184
  146.5 18.9 copy-start.12
  146.5 20.0 %copy-start.11 = (bf16[256,128]{0,1:T(8,128)(2,1)S(1)}, bf16[256,128]{0,1:T(8,128)(2,1)}, u32[]{:S(2)}) copy-start(bf16[256,128]{0,1:T(8,128)(2,1)} %slice.2555) | copy-start | bytes 196612 | tf_op jit(solution)/shard_map/while
  185.7 18.9 copy-start.12
  185.7 20.0 %copy-start.11 = (bf16[256,128]{0,1:T(8,128)(2,1)S(1)}, bf16[256,128]{0,1:T(8,128)(2,1)}, u32[]{:S(2)}) copy-start(bf16[256,128]{0,1:T(8,128)(2,1)} %slice.2555) | copy-start | bytes 196612 | tf_op jit(solution)/shard_map/while
  224.8 18.9 copy-start.12
  224.8 20.0 %copy-start.11 = (bf16[256,128]{0,1:T(8,128)(2,1)S(1)}, bf16[256,128]{0,1:T(8,128)(2,1)}, u32[]{:S(2)}) copy-start(bf16[256,128]{0,1:T(8,128)(2,1)} %slice.2555) | copy-start | bytes 196612 | tf_op jit(solution)/shard_map/while
  264.0 18.9 copy-start.12
  264.0 20.0 %copy-start.11 = (bf16[256,128]{0,1:T(8,128)(2,1)S(1)}, bf16[256,128]{0,1:T(8,128)(2,1)}, u32[]{:S(2)}) copy-start(bf16[256,128]{0,1:T(8,128)(2,1)} %slice.2555) | copy-start | bytes 196612 | tf_op jit(solution)/shard_map/while
  303.1 18.9 copy-start.12
  303.1 20.0 %copy-start.11 = (bf16[256,128]{0,1:T(8,128)(2,1)S(1)}, bf16[256,128]{0,1:T(8,128)(2,1)}, u32[]{:S(2)}) copy-start(bf16[256,128]{0,1:T(8,128)(2,1)} %slice.2555) | copy-start | bytes 196612 | tf_op jit(solution)/shard_map/while
  342.3 18.9 copy-start.12
  342.3 20.0 %copy-start.11 = (bf16[256,128]{0,1:T(8,128)(2,1)S(1)}, bf16[256,128]{0,1:T(8,128)(2,1)}, u32[]{:S(2)}) copy-start(bf16[256,128]{0,1:T(8,128)(2,1)} %slice.2555) | copy-start | bytes 196612 | tf_op jit(solution)/shard_map/while
  381.5 18.9 copy-start.12
  381.5 20.0 %copy-start.11 = (bf16[256,128]{0,1:T(8,128)(2,1)S(1)}, bf16[256,128]{0,1:T(8,128)(2,1)}, u32[]{:S(2)}) copy-start(bf16[256,128]{0,1:T(8,128)(2,1)} %slice.2555) | copy-start | bytes 196612 | tf_op jit(solution)/shard_map/while
  420.6 18.9 copy-start.12
  420.6 20.0 %copy-start.11 = (bf16[256,128]{0,1:T(8,128)(2,1)S(1)}, bf16[256,128]{0,1:T(8,128)(2,1)}, u32[]{:S(2)}) copy-start(bf16[256,128]{0,1:T(8,128)(2,1)} %slice.2555) | copy-start | bytes 196612 | tf_op jit(solution)/shard_map/while
  459.8 18.9 copy-start.12
  459.8 20.0 %copy-start.11 = (bf16[256,128]{0,1:T(8,128)(2,1)S(1)}, bf16[256,128]{0,1:T(8,128)(2,1)}, u32[]{:S(2)}) copy-start(bf16[256,128]{0,1:T(8,128)(2,1)} %slice.2555) | copy-start | bytes 196612 | tf_op jit(solution)/shard_map/while
  498.9 18.9 copy-start.12
  498.9 20.0 %copy-start.11 = (bf16[256,128]{0,1:T(8,128)(2,1)S(1)}, bf16[256,128]{0,1:T(8,128)(2,1)}, u32[]{:S(2)}) copy-start(bf16[256,128]{0,1:T(8,128)(2,1)} %slice.2555) | copy-start | bytes 196612 | tf_op jit(solution)/shard_map/while
  538.1 18.9 copy-start.12
  538.1 20.0 %copy-start.11 = (bf16[256,128]{0,1:T(8,128)(2,1)S(1)}, bf16[256,128]{0,1:T(8,128)(2,1)}, u32[]{:S(2)}) copy-start(bf16[256,128]{0,1:T(8,128)(2,1)} %slice.2555) | copy-start | bytes 196612 | tf_op jit(solution)/shard_map/while
  577.2 18.9 copy-start.12
  577.2 20.0 %copy-start.11 = (bf16[256,128]{0,1:T(8,128)(2,1)S(1)}, bf16[256,128]{0,1:T(8,128)(2,1)}, u32[]{:S(2)}) copy-start(bf16[256,128]{0,1:T(8,128)(2,1)} %slice.2555) | copy-start | bytes 196612 | tf_op jit(solution)/shard_map/while
  616.4 18.9 copy-start.12
  616.4 20.0 %copy-start.11 = (bf16[256,128]{0,1:T(8,128)(2,1)S(1)}, bf16[256,128]{0,1:T(8,128)(2,1)}, u32[]{:S(2)}) copy-start(bf16[256,128]{0,1:T(8,128)(2,1)} %slice.2555) | copy-start | bytes 196612 | tf_op jit(solution)/shard_map/while
  655.6 18.9 copy-start.12
  655.6 20.0 %copy-start.11 = (bf16[256,128]{0,1:T(8,128)(2,1)S(1)}, bf16[256,128]{0,1:T(8,128)(2,1)}, u32[]{:S(2)}) copy-start(bf16[256,128]{0,1:T(8,128)(2,1)} %slice.2555) | copy-start | bytes 196612 | tf_op jit(solution)/shard_map/while
  694.7 18.9 copy-start.12
  694.7 20.0 %copy-start.11 = (bf16[256,128]{0,1:T(8,128)(2,1)S(1)}, bf16[256,128]{0,1:T(8,128)(2,1)}, u32[]{:S(2)}) copy-start(bf16[256,128]{0,1:T(8,128)(2,1)} %slice.2555) | copy-start | bytes 196612 | tf_op jit(solution)/shard_map/while
  733.9 18.9 copy-start.12
  733.9 20.0 %copy-start.11 = (bf16[256,128]{0,1:T(8,128)(2,1)S(1)}, bf16[256,128]{0,1:T(8,128)(2,1)}, u32[]{:S(2)}) copy-start(bf16[256,128]{0,1:T(8,128)(2,1)} %slice.2555) | copy-start | bytes 196612 | tf_op jit(solution)/shard_map/while
  770.5 13.4 copy-start.7
  770.6 13.4 copy-start.45
  787.3 47.4 %all-gather.9.cloned.1.call-start = ((), (), s32[]{:S(2)}) async-start(), calls=%async_computation.15 | async-start | bytes 1310720 | tf_op jit(solution)/shard_map/all_gather | solution.py:196
  789.5 45.3 %copy-start.52 = (f32[1024]{0:T(1024)S(1)}, f32[1024]{0:T(1024)}, u32[]{:S(2)}) copy-start(f32[1024]{0:T(1024)} %param.100) | copy-start | bytes 12292
  789.5 77.6 %reduce-scatter.12.cloned.1.call-start = ((), (), s32[]{:S(2)}) async-start(), calls=%async_computation.16 | async-start | bytes 1310720 | tf_op jit(solution)/shard_map/reduce_scatter | solution.py:208
  843.1 50.2 %reduce-scatter.10.cloned.1.call-start = ((), (), s32[]{:S(2)}) async-start(), calls=%async_computation.14 | async-start | bytes 1310720 | tf_op jit(solution)/shard_map/reduce_scatter | solution.py:188
  847.2 46.1 %copy-start.47 = (f32[1024]{0:T(1024)S(1)}, f32[1024]{0:T(1024)}, u32[]{:S(2)}) copy-start(f32[1024]{0:T(1024)} %param.102) | copy-start | bytes 12292
  847.2 49.6 %copy-start.8 = (bf16[1024,1024]{1,0:T(8,128)(2,1)S(1)}, bf16[1024,1024]{1,0:T(8,128)(2,1)}, u32[]{:S(2)}) copy-start(bf16[1024,1024]{1,0:T(8,128)(2,1)} %param.95) | copy-start | bytes 6291460
  847.2 99.3 %all-gather.11.cloned.1.call-start = ((), (), s32[]{:S(2)}) async-start(), calls=%async_computation.17 | async-start | bytes 4456448 | tf_op jit(solution)/shard_map/all_gather | solution.py:273
  898.5 12.0 all-to-all-start.3
  902.9 8.3 copy-start.26
  902.9 510.3 %reduce-scatter.16.cloned.1.call-start = ((), (), s32[]{:S(2)}) async-start(), calls=%async_computation.19 | async-start | bytes 4456448 | tf_op jit(solution)/shard_map/reduce_scatter | solution.py:281
  1335.9 158.5 %reduce-scatter.14.cloned.1.call-start = ((), (), s32[]{:S(2)}) async-start(), calls=%async_computation.18 | async-start | bytes 4456448 | tf_op jit(solution)/shard_map/reduce_scatter | solution.py:278
  1342.4 270.6 %all-reduce.5.cloned.1.call-start = ((), (), s32[]{:S(2)}) async-start(), calls=%async_computation.23 | async-start | bytes 8388608 | tf_op jit(solution)/shard_map/psum | solution.py:329
  1497.2 24.5 %all-to-all-start.4 = ((bf16[3,1024,128]{2,0,1:T(4,128)(2,1)}), bf16[3,1024,128]{2,0,1:T(4,128)(2,1)S(1)}, u32[]{:S(2)}, u32[]{:S(2)}) async-start(bf16[3,1024,128]{2,0,1:T(4,128)(2,1)} %copy.305), calls=%async_computation.8 | async-start | bytes 2097152 | tf_op jit(solution)/shard_map/all_to_all | solution.py:286
  1501.7 191.7 %reduce-scatter.22.cloned.1.call-start = ((), (), s32[]{:S(2)}) async-start(), calls=%async_computation.22 | async-start | bytes 270336
  1501.7 21.2 %copy-start.35 = (f32[1024]{0:T(1024)S(1)}, f32[1024]{0:T(1024)}, u32[]{:S(2)}) copy-start(f32[1024]{0:T(1024)} %param.91) | copy-start | bytes 12292
  1501.7 21.2 %copy-start.40 = (f32[128]{0:T(128)S(1)}, f32[128]{0:T(128)}, u32[]{:S(2)}) copy-start(f32[128]{0:T(128)} %copy-done.39) | copy-start | bytes 1540
  1501.7 21.2 %copy-start.42 = (f32[128]{0:T(128)S(1)}, f32[128]{0:T(128)}, u32[]{:S(2)}) copy-start(f32[128]{0:T(128)} %copy-done.41) | copy-start | bytes 1540
  1528.8 246.3 %reduce-scatter.20.cloned.1.call-start = ((), (), s32[]{:S(2)}) async-start(), calls=%async_computation.21 | async-start | bytes 2162688 | tf_op jit(solution)/shard_map/reduce_scatter | solution.py:316
  1531.0 333.4 %reduce-scatter.18.cloned.1.call-start = ((), (), s32[]{:S(2)}) async-start(), calls=%async_computation.20 | async-start | bytes 6488064 | tf_op jit(solution)/shard_map/reduce_scatter | solution.py:313
  1536.3 371.5 %all-reduce.7.cloned.1.call-start = ((), (), s32[]{:S(2)}) async-start(), calls=%async_computation.24 | async-start | bytes 524288 | tf_op jit(solution)/shard_map/psum | solution.py:324
  1617.2 293.9 %copy-start.1 = (bf16[1024,1024]{1,0:T(8,128)(2,1)S(1)}, bf16[1024,1024]{1,0:T(8,128)(2,1)}, u32[]{:S(2)}) copy-start(bf16[1024,1024]{1,0:T(8,128)(2,1)} %param.101) | copy-start | bytes 6291460
  (308 other events, 929.6 us)
Sparse Core Ops, SparseCore 0:
  49.7 93.6 all-gather.4
  787.5 20.6 all-gather.6
  810.4 24.2 all-gather.8
  843.2 23.8 reduce-scatter.11
  870.0 23.1 reduce-scatter.9
  895.2 51.2 all-gather.10
  1336.0 77.1 reduce-scatter.15
  1417.5 76.8 reduce-scatter.13
  1498.4 114.4 all-reduce.4
  1616.8 76.5 reduce-scatter.21
  1696.9 78.1 reduce-scatter.19
  1778.7 85.5 reduce-scatter.17
  1866.9 40.8 all-reduce.6
